TPU v7x, 512 devices: a whole 4x4x16 slice. The times are simulated.
512 devices in a mesh: req: 16 (over z), ctx: 32 (over x, y, core).
Axes of the slice: x: 4, y: 4, z: 16, core: 2. Of those that a mesh axis runs over, the one named last changes fastest.
Arguments:
- query_rows: bfloat16 [131072, 1024], P(('req', 'ctx')), parts along dimension 0, may hold values from -8 to 8
- key_rows: bfloat16 [131072, 128], P(('req', 'ctx')), parts along dimension 0, may hold values from -8 to 8
- value_rows: bfloat16 [131072, 128], P(('req', 'ctx')), parts along dimension 0, may hold values from -8 to 8
- document_ids: int32 [131072], P('req'), parts along dimension 0, may hold values from 0 to 7, never falling along the last dimension, each value on 1 to 4096 neighbouring positions
Outputs:
- attended: bfloat16 [131072, 1024], P(('req', 'ctx')), parts along dimension 0
There are 16 independent parts, one for each index of `req`. A program takes and returns all parts, laid end to end along the dimension named above; each array names one. Nothing has to cross between parts.
All inputs are finite; a program needn't handle non-finite values.
Results may differ from a plain program's by a relative error of at most 0.004.
Values may be sent and summed in bfloat16 or wider, within the bound.
No kernel may reach another device: no remote copies, remote signals or barrier semaphores. Data moves between devices by JAX's collectives and lax.ppermute only.
A program may use at most 64 MiB of HBM per device.

v0:
```python
import math
import jax
import jax.numpy as jnp
from jax import lax
from jax.sharding import PartitionSpec as P


def make_absorb(stacked, positions, query_docs, document_ids):
    dim_size = stacked.shape[2]
    factor = 1.0 / math.sqrt(dim_size)

    def absorb(carry, piece, start, valid):
        key_piece, value_piece = piece
        length = key_piece.shape[0]
        block = math.gcd(length, 512)

        def one_block(state, which):
            offset = which * block
            key_block = lax.dynamic_slice_in_dim(key_piece, offset, block, 0)
            value_block = lax.dynamic_slice_in_dim(value_piece, offset, block, 0)
            key_positions = offset + jnp.arange(block, dtype=jnp.int32)
            key_docs = lax.dynamic_slice_in_dim(document_ids, jnp.maximum(offset, 0), block, 0)
            allowed = (
                valid
                & (query_docs[:, None] == key_docs[None, :])
                & (key_positions[None, :] <= positions[:, None])
            )

            def compute(inner):
                running, totals, accum = inner
                scores = (
                    jnp.einsum(
                        "thd,sd->ths", stacked, key_block, preferred_element_type=jnp.float32
                    )
                    * factor
                )
                masked = jnp.where(allowed[:, None, :], scores, jnp.float32(-1e30))
                newest = jnp.maximum(running, jnp.max(masked, axis=-1))
                weights = jnp.where(
                    allowed[:, None, :], jnp.exp(masked - newest[..., None]), jnp.float32(0.0)
                )
                shrink = jnp.exp(running - newest)
                totals = totals * shrink + jnp.sum(weights, axis=-1)
                accum = accum * shrink[..., None] + jnp.einsum(
                    "ths,sd->thd",
                    weights.astype(jnp.bfloat16),
                    value_block,
                    preferred_element_type=jnp.float32,
                )
                return (newest, totals, accum)

            def unchanged(inner):
                return inner

            return (lax.cond(jnp.any(allowed), compute, unchanged, state), None)

        result, _ = lax.scan(one_block, carry, jnp.arange(length // block, dtype=jnp.int32))
        return result

    return absorb


def start_state(stacked):
    count, head_count, dim_size = stacked.shape
    return (
        jnp.full((count, head_count), -1e30, jnp.float32),
        jnp.zeros((count, head_count), jnp.float32),
        jnp.zeros((count, head_count, dim_size), jnp.float32),
    )


def finish(state):
    running, totals, accum = state
    result = accum / totals[..., None]
    count = result.shape[0]
    return result.reshape(count, result.shape[1] * result.shape[2]).astype(jnp.bfloat16)


def split_heads(active, dim_size):
    count = active.shape[0]
    return active.reshape(count, active.shape[1] // dim_size, dim_size)


def on_device(query_rows, key_rows, value_rows, document_ids):
    local_rows = query_rows.shape[0]
    dim_size = key_rows.shape[1]
    device = lax.axis_index("ctx")
    offsets = jnp.arange(local_rows, dtype=jnp.int32)
    own_positions = device * local_rows + offsets
    query_docs = jnp.take(document_ids, own_positions)
    stacked = split_heads(query_rows, dim_size)
    absorb = make_absorb(stacked, own_positions, query_docs, document_ids)
    start = jnp.int32(0)
    state = absorb(
        start_state(stacked),
        (
            lax.all_gather(key_rows, "ctx", axis=0, tiled=True),
            lax.all_gather(value_rows, "ctx", axis=0, tiled=True),
        ),
        start,
        start >= 0,
    )
    attended = finish(state)
    return attended


def solution(mesh):
    in_specs = (P(("req", "ctx"), None), P(("req", "ctx"), None), P(("req", "ctx"), None), P("req"))
    out_specs = P(("req", "ctx"), None)
    return jax.shard_map(
        on_device, mesh=mesh, in_specs=in_specs, out_specs=out_specs, check_vma=False
    )
```

profile of v0, /device:TPU:4, one launch (start us, length us, event | category | flops | bytes accessed | tf_op | source)
XLA Modules:
  0.0 247.9 jit_solution(16759929622175136257)
XLA Ops:
  8.0 1.2 copy.8
  9.6 2.0 gather_fusion
  11.6 61.7 %all-gather.3.cloned.1.call-done = bf16[8192,128]{1,0:T(8,128)(2,1)} async-done(((bf16[256,128]{1,0:T(8,128)(2,1)}), bf16[8192,128]{1,0:T(8,128)(2,1)}) %all-gather.3.cloned.1.call-update) | async-done | bytes 2097168 | tf_op jit(solution)/shard_map/all_gather | solution.py:97
  73.3 61.5 %all-gather.5.cloned.1.call-done = bf16[8192,128]{1,0:T(8,128)(2,1)} async-done(((bf16[256,128]{1,0:T(8,128)(2,1)}), bf16[8192,128]{1,0:T(8,128)(2,1)}) %all-gather.5.cloned.1.call-update) | async-done | bytes 2097168 | tf_op jit(solution)/shard_map/all_gather | solution.py:98
  134.8 105.0 %while.15 = (s32[]{:T(128)}, f32[256,8]{0,1:T(8,128)S(1)}, f32[256,8]{0,1:T(8,128)S(1)}, f32[256,8,128]{2,0,1:T(8,128)S(1)}, s32[256]{0:T(256)S(1)}, /*index=5*/...) while((s32[]{:T(128)}, f32[256,8]{0,1:T(8,128)S(1)}, ...), condition=%wide.region_6.7_spmd.clone, body=%wide.region_0.6_spmd.clone.sunk | while | flops 551555840 | bytes 16135525 | solution.py:57
  136.9 0.8 fusion.26
  138.4 5.4 %conditional.3 = ((f32[256,8]{0,1:T(8,128)S(1)}, f32[256,8]{0,1:T(8,128)S(1)}, f32[256,8,128]{2,0,1:T(8,128)S(1)})) conditional(s32[]{:T(128)} %convert_element_type.27, (f32[256,8]{0,1:T(8,128)S(1)}, f32[256,8]{0,1:T(8,128)S(1)}, f32[256,8,128]{2,0,1:T(8,128)S(1)}) %tuple.45, (pred[256,512]{0,1:T(8,128)(4,1)S(1)}, s32[]{:T(128)}, ...), branch_computations={%region_2.2_spmd, %region_3.5_spmd} | conditional | flops 551030784 | bytes 15990858 | solution.py:55
  138.4 1.7 fusion.2
  140.1 1.0 fusion.4
  141.2 2.6 %fusion.8 = f32[256,8,128]{2,0,1:T(8,128)S(1)} fusion(f32[512,256,8]{1,0,2:T(8,128)S(1)} %get-tuple-element.234, f32[256,8]{0,1:T(8,128)S(1)} %max.7, pred[256,512]{0,1:T(8,128)(4,1)S(1)} %get-tuple-element.142, f32[256,8,128]{2,0,1:T(8,128)S(1)} %get-tuple-element.147, f32[256,8]{0,1:T(8,128)S(1)} %get-tuple-element.230, ...), kind=kOutput, calls=%fused_computation.9 | convolution fusion | flops 274202624 | bytes 6569988 | tf_op jit(solution)/shard_map/while/body/eval_jaxpr/cond/branch_1_fun/ths,sd->thd/dot_general | solution.py:44
  145.8 0.8 fusion.26
  147.3 5.4 %conditional.3 = ((f32[256,8]{0,1:T(8,128)S(1)}, f32[256,8]{0,1:T(8,128)S(1)}, f32[256,8,128]{2,0,1:T(8,128)S(1)})) conditional(s32[]{:T(128)} %convert_element_type.27, (f32[256,8]{0,1:T(8,128)S(1)}, f32[256,8]{0,1:T(8,128)S(1)}, f32[256,8,128]{2,0,1:T(8,128)S(1)}) %tuple.45, (pred[256,512]{0,1:T(8,128)(4,1)S(1)}, s32[]{:T(128)}, ...), branch_computations={%region_2.2_spmd, %region_3.5_spmd} | conditional | flops 551030784 | bytes 15990858 | solution.py:55
  147.3 1.7 fusion.2
  149.1 1.0 fusion.4
  150.1 2.6 %fusion.8 = f32[256,8,128]{2,0,1:T(8,128)S(1)} fusion(f32[512,256,8]{1,0,2:T(8,128)S(1)} %get-tuple-element.234, f32[256,8]{0,1:T(8,128)S(1)} %max.7, pred[256,512]{0,1:T(8,128)(4,1)S(1)} %get-tuple-element.142, f32[256,8,128]{2,0,1:T(8,128)S(1)} %get-tuple-element.147, f32[256,8]{0,1:T(8,128)S(1)} %get-tuple-element.230, ...), kind=kOutput, calls=%fused_computation.9 | convolution fusion | flops 274202624 | bytes 6569988 | tf_op jit(solution)/shard_map/while/body/eval_jaxpr/cond/branch_1_fun/ths,sd->thd/dot_general | solution.py:44
  154.0 0.8 dynamic_slice.40
  154.7 0.8 fusion.26
  156.2 5.4 %conditional.3 = ((f32[256,8]{0,1:T(8,128)S(1)}, f32[256,8]{0,1:T(8,128)S(1)}, f32[256,8,128]{2,0,1:T(8,128)S(1)})) conditional(s32[]{:T(128)} %convert_element_type.27, (f32[256,8]{0,1:T(8,128)S(1)}, f32[256,8]{0,1:T(8,128)S(1)}, f32[256,8,128]{2,0,1:T(8,128)S(1)}) %tuple.45, (pred[256,512]{0,1:T(8,128)(4,1)S(1)}, s32[]{:T(128)}, ...), branch_computations={%region_2.2_spmd, %region_3.5_spmd} | conditional | flops 551030784 | bytes 15990858 | solution.py:55
  156.2 1.7 fusion.2
  158.0 1.0 fusion.4
  159.0 2.6 %fusion.8 = f32[256,8,128]{2,0,1:T(8,128)S(1)} fusion(f32[512,256,8]{1,0,2:T(8,128)S(1)} %get-tuple-element.234, f32[256,8]{0,1:T(8,128)S(1)} %max.7, pred[256,512]{0,1:T(8,128)(4,1)S(1)} %get-tuple-element.142, f32[256,8,128]{2,0,1:T(8,128)S(1)} %get-tuple-element.147, f32[256,8]{0,1:T(8,128)S(1)} %get-tuple-element.230, ...), kind=kOutput, calls=%fused_computation.9 | convolution fusion | flops 274202624 | bytes 6569988 | tf_op jit(solution)/shard_map/while/body/eval_jaxpr/cond/branch_1_fun/ths,sd->thd/dot_general | solution.py:44
  162.9 0.8 dynamic_slice.40
  163.7 0.8 fusion.26
  165.1 5.4 %conditional.3 = ((f32[256,8]{0,1:T(8,128)S(1)}, f32[256,8]{0,1:T(8,128)S(1)}, f32[256,8,128]{2,0,1:T(8,128)S(1)})) conditional(s32[]{:T(128)} %convert_element_type.27, (f32[256,8]{0,1:T(8,128)S(1)}, f32[256,8]{0,1:T(8,128)S(1)}, f32[256,8,128]{2,0,1:T(8,128)S(1)}) %tuple.45, (pred[256,512]{0,1:T(8,128)(4,1)S(1)}, s32[]{:T(128)}, ...), branch_computations={%region_2.2_spmd, %region_3.5_spmd} | conditional | flops 551030784 | bytes 15990858 | solution.py:55
  165.2 1.7 fusion.2
  166.9 1.0 fusion.4
  167.9 2.6 %fusion.8 = f32[256,8,128]{2,0,1:T(8,128)S(1)} fusion(f32[512,256,8]{1,0,2:T(8,128)S(1)} %get-tuple-element.234, f32[256,8]{0,1:T(8,128)S(1)} %max.7, pred[256,512]{0,1:T(8,128)(4,1)S(1)} %get-tuple-element.142, f32[256,8,128]{2,0,1:T(8,128)S(1)} %get-tuple-element.147, f32[256,8]{0,1:T(8,128)S(1)} %get-tuple-element.230, ...), kind=kOutput, calls=%fused_computation.9 | convolution fusion | flops 274202624 | bytes 6569988 | tf_op jit(solution)/shard_map/while/body/eval_jaxpr/cond/branch_1_fun/ths,sd->thd/dot_general | solution.py:44
  171.8 0.8 dynamic_slice.40
  172.6 0.8 fusion.26
  174.1 5.4 %conditional.3 = ((f32[256,8]{0,1:T(8,128)S(1)}, f32[256,8]{0,1:T(8,128)S(1)}, f32[256,8,128]{2,0,1:T(8,128)S(1)})) conditional(s32[]{:T(128)} %convert_element_type.27, (f32[256,8]{0,1:T(8,128)S(1)}, f32[256,8]{0,1:T(8,128)S(1)}, f32[256,8,128]{2,0,1:T(8,128)S(1)}) %tuple.45, (pred[256,512]{0,1:T(8,128)(4,1)S(1)}, s32[]{:T(128)}, ...), branch_computations={%region_2.2_spmd, %region_3.5_spmd} | conditional | flops 551030784 | bytes 15990858 | solution.py:55
  174.1 1.7 fusion.2
  175.8 1.0 fusion.4
  176.9 2.6 %fusion.8 = f32[256,8,128]{2,0,1:T(8,128)S(1)} fusion(f32[512,256,8]{1,0,2:T(8,128)S(1)} %get-tuple-element.234, f32[256,8]{0,1:T(8,128)S(1)} %max.7, pred[256,512]{0,1:T(8,128)(4,1)S(1)} %get-tuple-element.142, f32[256,8,128]{2,0,1:T(8,128)S(1)} %get-tuple-element.147, f32[256,8]{0,1:T(8,128)S(1)} %get-tuple-element.230, ...), kind=kOutput, calls=%fused_computation.9 | convolution fusion | flops 274202624 | bytes 6569988 | tf_op jit(solution)/shard_map/while/body/eval_jaxpr/cond/branch_1_fun/ths,sd->thd/dot_general | solution.py:44
  181.5 0.8 fusion.26
  183.0 5.4 %conditional.3 = ((f32[256,8]{0,1:T(8,128)S(1)}, f32[256,8]{0,1:T(8,128)S(1)}, f32[256,8,128]{2,0,1:T(8,128)S(1)})) conditional(s32[]{:T(128)} %convert_element_type.27, (f32[256,8]{0,1:T(8,128)S(1)}, f32[256,8]{0,1:T(8,128)S(1)}, f32[256,8,128]{2,0,1:T(8,128)S(1)}) %tuple.45, (pred[256,512]{0,1:T(8,128)(4,1)S(1)}, s32[]{:T(128)}, ...), branch_computations={%region_2.2_spmd, %region_3.5_spmd} | conditional | flops 551030784 | bytes 15990858 | solution.py:55
  183.0 1.7 fusion.2
  184.8 1.0 fusion.4
  185.8 2.6 %fusion.8 = f32[256,8,128]{2,0,1:T(8,128)S(1)} fusion(f32[512,256,8]{1,0,2:T(8,128)S(1)} %get-tuple-element.234, f32[256,8]{0,1:T(8,128)S(1)} %max.7, pred[256,512]{0,1:T(8,128)(4,1)S(1)} %get-tuple-element.142, f32[256,8,128]{2,0,1:T(8,128)S(1)} %get-tuple-element.147, f32[256,8]{0,1:T(8,128)S(1)} %get-tuple-element.230, ...), kind=kOutput, calls=%fused_computation.9 | convolution fusion | flops 274202624 | bytes 6569988 | tf_op jit(solution)/shard_map/while/body/eval_jaxpr/cond/branch_1_fun/ths,sd->thd/dot_general | solution.py:44
  189.7 0.8 dynamic_slice.40
  190.4 0.8 fusion.26
  191.9 5.4 %conditional.3 = ((f32[256,8]{0,1:T(8,128)S(1)}, f32[256,8]{0,1:T(8,128)S(1)}, f32[256,8,128]{2,0,1:T(8,128)S(1)})) conditional(s32[]{:T(128)} %convert_element_type.27, (f32[256,8]{0,1:T(8,128)S(1)}, f32[256,8]{0,1:T(8,128)S(1)}, f32[256,8,128]{2,0,1:T(8,128)S(1)}) %tuple.45, (pred[256,512]{0,1:T(8,128)(4,1)S(1)}, s32[]{:T(128)}, ...), branch_computations={%region_2.2_spmd, %region_3.5_spmd} | conditional | flops 551030784 | bytes 15990858 | solution.py:55
  191.9 1.7 fusion.2
  193.7 1.0 fusion.4
  194.7 2.6 %fusion.8 = f32[256,8,128]{2,0,1:T(8,128)S(1)} fusion(f32[512,256,8]{1,0,2:T(8,128)S(1)} %get-tuple-element.234, f32[256,8]{0,1:T(8,128)S(1)} %max.7, pred[256,512]{0,1:T(8,128)(4,1)S(1)} %get-tuple-element.142, f32[256,8,128]{2,0,1:T(8,128)S(1)} %get-tuple-element.147, f32[256,8]{0,1:T(8,128)S(1)} %get-tuple-element.230, ...), kind=kOutput, calls=%fused_computation.9 | convolution fusion | flops 274202624 | bytes 6569988 | tf_op jit(solution)/shard_map/while/body/eval_jaxpr/cond/branch_1_fun/ths,sd->thd/dot_general | solution.py:44
  198.6 0.8 dynamic_slice.40
  199.4 0.8 fusion.26
  200.8 5.4 %conditional.3 = ((f32[256,8]{0,1:T(8,128)S(1)}, f32[256,8]{0,1:T(8,128)S(1)}, f32[256,8,128]{2,0,1:T(8,128)S(1)})) conditional(s32[]{:T(128)} %convert_element_type.27, (f32[256,8]{0,1:T(8,128)S(1)}, f32[256,8]{0,1:T(8,128)S(1)}, f32[256,8,128]{2,0,1:T(8,128)S(1)}) %tuple.45, (pred[256,512]{0,1:T(8,128)(4,1)S(1)}, s32[]{:T(128)}, ...), branch_computations={%region_2.2_spmd, %region_3.5_spmd} | conditional | flops 551030784 | bytes 15990858 | solution.py:55
  200.9 1.7 fusion.2
  202.6 1.0 fusion.4
  203.6 2.6 %fusion.8 = f32[256,8,128]{2,0,1:T(8,128)S(1)} fusion(f32[512,256,8]{1,0,2:T(8,128)S(1)} %get-tuple-element.234, f32[256,8]{0,1:T(8,128)S(1)} %max.7, pred[256,512]{0,1:T(8,128)(4,1)S(1)} %get-tuple-element.142, f32[256,8,128]{2,0,1:T(8,128)S(1)} %get-tuple-element.147, f32[256,8]{0,1:T(8,128)S(1)} %get-tuple-element.230, ...), kind=kOutput, calls=%fused_computation.9 | convolution fusion | flops 274202624 | bytes 6569988 | tf_op jit(solution)/shard_map/while/body/eval_jaxpr/cond/branch_1_fun/ths,sd->thd/dot_general | solution.py:44
  207.5 0.8 dynamic_slice.40
  208.3 0.8 fusion.26
  209.8 5.4 %conditional.3 = ((f32[256,8]{0,1:T(8,128)S(1)}, f32[256,8]{0,1:T(8,128)S(1)}, f32[256,8,128]{2,0,1:T(8,128)S(1)})) conditional(s32[]{:T(128)} %convert_element_type.27, (f32[256,8]{0,1:T(8,128)S(1)}, f32[256,8]{0,1:T(8,128)S(1)}, f32[256,8,128]{2,0,1:T(8,128)S(1)}) %tuple.45, (pred[256,512]{0,1:T(8,128)(4,1)S(1)}, s32[]{:T(128)}, ...), branch_computations={%region_2.2_spmd, %region_3.5_spmd} | conditional | flops 551030784 | bytes 15990858 | solution.py:55
  209.8 1.7 fusion.2
  211.5 1.0 fusion.4
  212.6 2.6 %fusion.8 = f32[256,8,128]{2,0,1:T(8,128)S(1)} fusion(f32[512,256,8]{1,0,2:T(8,128)S(1)} %get-tuple-element.234, f32[256,8]{0,1:T(8,128)S(1)} %max.7, pred[256,512]{0,1:T(8,128)(4,1)S(1)} %get-tuple-element.142, f32[256,8,128]{2,0,1:T(8,128)S(1)} %get-tuple-element.147, f32[256,8]{0,1:T(8,128)S(1)} %get-tuple-element.230, ...), kind=kOutput, calls=%fused_computation.9 | convolution fusion | flops 274202624 | bytes 6569988 | tf_op jit(solution)/shard_map/while/body/eval_jaxpr/cond/branch_1_fun/ths,sd->thd/dot_general | solution.py:44
  217.2 0.8 fusion.26
  220.8 0.8 fusion.26
  224.3 0.8 fusion.26
  227.8 0.8 fusion.26
  231.4 0.8 fusion.26
  234.9 0.8 fusion.26
  238.4 0.8 fusion.26
  239.9 1.1 copy_bitcast_fusion
  (104 shorter events, 19.8 us)
Async XLA Ops:
  6.5 66.7 %all-gather.3.cloned.1.call-start = ((), (), s32[]{:S(2)}) async-start(), calls=%async_computation | async-start | bytes 2162688 | tf_op jit(solution)/shard_map/all_gather | solution.py:97
  7.3 127.5 %all-gather.5.cloned.1.call-start = ((), (), s32[]{:S(2)}) async-start(), calls=%async_computation.1 | async-start | bytes 2162688 | tf_op jit(solution)/shard_map/all_gather | solution.py:98
Sparse Core Ops, SparseCore 0:
  10.5 62.7 all-gather.2
  76.4 58.3 all-gather.4
where the time goes:
time: 250 us; the launch traced here: 248 us
  waiting for transfers between devices  125 us (50%)
  matrix products  38.9 us (16%)
  local copies, waits for them, and re-layouts  25.9 us (10%)
  other arithmetic  24 us (10%)
  loops' own time  21 us (8%)
  between operations  13.4 us (5%)
    all_gather x1, waiting for transfers between devices, on_device(): lax.all_gather(key_rows, 'ctx', axis=0, tiled=True)  61.7 us
    all_gather x1, waiting for transfers between devices, on_device(): lax.all_gather(value_rows, 'ctx', axis=0, tiled=True)  61.5 us
    dot_general x9, matrix products, compute(): jnp.einsum('ths,sd->thd', weights.astype(jnp.bfloat16), value_block, pref...  23.3 us
    another operation x1, loops' own time, absorb(): lax.scan(one_block, carry, jnp.arange(length // block, dtype=jnp.int32))  20.3 us
    dot_general x9, matrix products, compute(): jnp.einsum('thd,sd->ths', stacked, key_block, preferred_element_type=jnp....  15.5 us
    reduce_or x16, other arithmetic, one_block(): return (lax.cond(jnp.any(allowed), compute, unchanged, state), None)  13.5 us
    dynamic_slice x16, local copies, waits for them, and re-layouts, one_block(): lax.dynamic_slice_in_dim(document_ids, jnp.maximum(offset, 0), block, 0)  12.5 us
    dynamic_slice x16, local copies, waits for them, and re-layouts, absorb(): lax.scan(one_block, carry, jnp.arange(length // block, dtype=jnp.int32))  9.88 us
  transfers between devices with their start and end apart: 2, of which 2 were waited for; matrix products, arithmetic and copies ran while one was open for 1% of the time, Pallas kernels for 0%

commit v1 on v0

--- a/solution.py
+++ b/solution.py
@@ -3,6 +3,13 @@
 import jax.numpy as jnp
 from jax import lax
 from jax.sharding import PartitionSpec as P
+
+
+def all_by_exchange(x, axis, along):
+    peers = lax.axis_size(axis)
+    pieces = jnp.stack([x for _ in range(peers)])
+    pieces = lax.all_to_all(pieces, axis, split_axis=0, concat_axis=0)
+    return jnp.concatenate(pieces, axis=along)
 
 
 def make_absorb(stacked, positions, query_docs, document_ids):
@@ -94,7 +101,7 @@
     state = absorb(
         start_state(stacked),
         (
-            lax.all_gather(key_rows, "ctx", axis=0, tiled=True),
+            all_by_exchange(key_rows, "ctx", 0),
             lax.all_gather(value_rows, "ctx", axis=0, tiled=True),
         ),
         start,

time: 250 us -> 182 us (0.73)
  waiting for transfers between devices: 125 us -> 57 us
  starting transfers between devices: 0.04 us -> 10.3 us
  local copies, waits for them, and re-layouts: 25.9 us -> 16.1 us
    all_gather x1 -> x0, waiting for transfers between devices: 61.7 us -> none  [on_device(): lax.all_gather(key_rows, 'ctx', axis=0, tiled=True)]
    all_gather x1, waiting for transfers between devices: 61.5 us -> 32.2 us  [on_device(): lax.all_gather(value_rows, 'ctx', axis=0, tiled=True)]
    all_to_all x0 -> x1, waiting for transfers between devices: none -> 24.1 us  [all_by_exchange(): pieces = lax.all_to_all(pieces, axis, split_axis=0, concat_axis=0)]
    dynamic_slice x16, local copies, waits for them, and re-layouts: 12.5 us -> 1.3 us  [one_block(): lax.dynamic_slice_in_dim(document_ids, jnp.maximum(offset, 0), block, 0)]
    all_to_all x0 -> x1, starting transfers between devices: none -> 10.3 us  [all_by_exchange(): pieces = lax.all_to_all(pieces, axis, split_axis=0, concat_axis=0)]
    another operation x0 -> x1, local copies, waits for them, and re-layouts: none -> 2.64 us  [all_by_exchange(): pieces = jnp.stack([x for _ in range(peers)])]
  transfers between devices with their start and end apart: 2 -> 2, of which waited for: 2 -> 2; matrix products, arithmetic and copies ran while one was open for 1% -> 3% of each run, Pallas kernels for 0% -> 0%
where the time goes in v1:
time: 182 us; the launch traced here: 181 us
  waiting for transfers between devices  57 us (31%)
  matrix products  38.9 us (21%)
  other arithmetic  24 us (13%)
  loops' own time  21 us (12%)
  local copies, waits for them, and re-layouts  16.1 us (9%)
  between operations  13.5 us (7%)
  starting transfers between devices  10.3 us (6%)
    all_gather x1, waiting for transfers between devices, on_device(): lax.all_gather(value_rows, 'ctx', axis=0, tiled=True)  32.2 us
    all_to_all x1, waiting for transfers between devices, all_by_exchange(): pieces = lax.all_to_all(pieces, axis, split_axis=0, concat_axis=0)  24.1 us
    dot_general x9, matrix products, compute(): jnp.einsum('ths,sd->thd', weights.astype(jnp.bfloat16), value_block, pref...  23.4 us
    another operation x1, loops' own time, absorb(): lax.scan(one_block, carry, jnp.arange(length // block, dtype=jnp.int32))  20.3 us
    dot_general x9, matrix products, compute(): jnp.einsum('thd,sd->ths', stacked, key_block, preferred_element_type=jnp....  15.6 us
    reduce_or x16, other arithmetic, one_block(): return (lax.cond(jnp.any(allowed), compute, unchanged, state), None)  13.5 us
    all_to_all x1, starting transfers between devices, all_by_exchange(): pieces = lax.all_to_all(pieces, axis, split_axis=0, concat_axis=0)  10.3 us
    dynamic_slice x16, local copies, waits for them, and re-layouts, absorb(): lax.scan(one_block, carry, jnp.arange(length // block, dtype=jnp.int32))  9.88 us
  transfers between devices with their start and end apart: 2, of which 2 were waited for; matrix products, arithmetic and copies ran while one was open for 3% of the time, Pallas kernels for 0%

profile of v1, /device:TPU:4, one launch (start us, length us, event | category | flops | bytes accessed | tf_op | source)
XLA Modules:
  0.0 180.8 jit_solution(8498864407674787726)
XLA Ops:
  6.5 0.7 all-gather.2.cloned.1.call-update
  7.3 2.6 %stack.2 = bf16[32,256,128]{2,1,0:T(8,128)(2,1)} broadcast(bf16[256,128]{1,0:T(8,128)(2,1)} %param.9), dimensions={1,2} | broadcast | bytes 2162688 | tf_op jit(solution)/shard_map/stack | solution.py:10
  9.9 10.3 %all-to-all-start = ((bf16[32,256,128]{2,1,0:T(8,128)(2,1)}), bf16[32,256,128]{2,1,0:T(8,128)(2,1)}, u32[]{:S(2)}, u32[]{:S(2)}) async-start(bf16[32,256,128]{2,1,0:T(8,128)(2,1)} %stack.2), calls=%async_computation | async-start | bytes 4194304 | tf_op jit(solution)/shard_map/all_to_all | solution.py:11
  20.7 1.7 gather_fusion
  22.5 24.1 %all-to-all-done = bf16[32,256,128]{2,1,0:T(8,128)(2,1)} async-done(((bf16[32,256,128]{2,1,0:T(8,128)(2,1)}), bf16[32,256,128]{2,1,0:T(8,128)(2,1)}, u32[]{:S(2)}, u32[]{:S(2)}) %all-to-all-start) | async-done | bytes 2097184 | tf_op jit(solution)/shard_map/all_to_all | solution.py:11
  46.6 32.2 %all-gather.2.cloned.1.call-done = bf16[8192,128]{1,0:T(8,128)(2,1)} async-done(((bf16[256,128]{1,0:T(8,128)(2,1)}), bf16[8192,128]{1,0:T(8,128)(2,1)}) %all-gather.2.cloned.1.call-update) | async-done | bytes 2097168 | tf_op jit(solution)/shard_map/all_gather | solution.py:105
  78.9 94.0 %while.15 = (s32[]{:T(128)}, f32[256,8]{0,1:T(8,128)S(1)}, f32[256,8]{0,1:T(8,128)S(1)}, f32[256,8,128]{2,0,1:T(8,128)S(1)}, s32[256]{0:T(256)S(1)}, /*index=5*/...) while((s32[]{:T(128)}, f32[256,8]{0,1:T(8,128)S(1)}, ...), condition=%wide.region_6.7_spmd.clone, body=%wide.region_0.6_spmd.clone.sunk | while | flops 551555840 | bytes 16135525 | solution.py:64
  80.2 0.8 fusion.26
  81.7 5.4 %conditional.3 = ((f32[256,8]{0,1:T(8,128)S(1)}, f32[256,8]{0,1:T(8,128)S(1)}, f32[256,8,128]{2,0,1:T(8,128)S(1)})) conditional(s32[]{:T(128)} %convert_element_type.27, (f32[256,8]{0,1:T(8,128)S(1)}, f32[256,8]{0,1:T(8,128)S(1)}, f32[256,8,128]{2,0,1:T(8,128)S(1)}) %tuple.45, (pred[256,512]{0,1:T(8,128)(4,1)S(1)}, s32[]{:T(128)}, ...), branch_computations={%region_2.2_spmd, %region_3.5_spmd} | conditional | flops 551030784 | bytes 15990858 | solution.py:62
  81.7 1.7 fusion.2
  83.4 1.0 fusion.4
  84.5 2.6 %fusion.8 = f32[256,8,128]{2,0,1:T(8,128)S(1)} fusion(f32[512,256,8]{1,0,2:T(8,128)S(1)} %get-tuple-element.234, f32[256,8]{0,1:T(8,128)S(1)} %max.7, pred[256,512]{0,1:T(8,128)(4,1)S(1)} %get-tuple-element.142, f32[256,8,128]{2,0,1:T(8,128)S(1)} %get-tuple-element.147, f32[256,8]{0,1:T(8,128)S(1)} %get-tuple-element.230, ...), kind=kOutput, calls=%fused_computation.9 | convolution fusion | flops 274202624 | bytes 6569988 | tf_op jit(solution)/shard_map/while/body/eval_jaxpr/cond/branch_1_fun/ths,sd->thd/dot_general | solution.py:51
  88.4 0.8 fusion.26
  89.9 5.4 %conditional.3 = ((f32[256,8]{0,1:T(8,128)S(1)}, f32[256,8]{0,1:T(8,128)S(1)}, f32[256,8,128]{2,0,1:T(8,128)S(1)})) conditional(s32[]{:T(128)} %convert_element_type.27, (f32[256,8]{0,1:T(8,128)S(1)}, f32[256,8]{0,1:T(8,128)S(1)}, f32[256,8,128]{2,0,1:T(8,128)S(1)}) %tuple.45, (pred[256,512]{0,1:T(8,128)(4,1)S(1)}, s32[]{:T(128)}, ...), branch_computations={%region_2.2_spmd, %region_3.5_spmd} | conditional | flops 551030784 | bytes 15990858 | solution.py:62
  89.9 1.7 fusion.2
  91.7 1.0 fusion.4
  92.7 2.6 %fusion.8 = f32[256,8,128]{2,0,1:T(8,128)S(1)} fusion(f32[512,256,8]{1,0,2:T(8,128)S(1)} %get-tuple-element.234, f32[256,8]{0,1:T(8,128)S(1)} %max.7, pred[256,512]{0,1:T(8,128)(4,1)S(1)} %get-tuple-element.142, f32[256,8,128]{2,0,1:T(8,128)S(1)} %get-tuple-element.147, f32[256,8]{0,1:T(8,128)S(1)} %get-tuple-element.230, ...), kind=kOutput, calls=%fused_computation.9 | convolution fusion | flops 274202624 | bytes 6569988 | tf_op jit(solution)/shard_map/while/body/eval_jaxpr/cond/branch_1_fun/ths,sd->thd/dot_general | solution.py:51
  95.3 0.6 dynamic_slice.39
  96.7 0.8 fusion.26
  98.1 5.4 %conditional.3 = ((f32[256,8]{0,1:T(8,128)S(1)}, f32[256,8]{0,1:T(8,128)S(1)}, f32[256,8,128]{2,0,1:T(8,128)S(1)})) conditional(s32[]{:T(128)} %convert_element_type.27, (f32[256,8]{0,1:T(8,128)S(1)}, f32[256,8]{0,1:T(8,128)S(1)}, f32[256,8,128]{2,0,1:T(8,128)S(1)}) %tuple.45, (pred[256,512]{0,1:T(8,128)(4,1)S(1)}, s32[]{:T(128)}, ...), branch_computations={%region_2.2_spmd, %region_3.5_spmd} | conditional | flops 551030784 | bytes 15990858 | solution.py:62
  98.2 1.7 fusion.2
  99.9 1.0 fusion.4
  100.9 2.6 %fusion.8 = f32[256,8,128]{2,0,1:T(8,128)S(1)} fusion(f32[512,256,8]{1,0,2:T(8,128)S(1)} %get-tuple-element.234, f32[256,8]{0,1:T(8,128)S(1)} %max.7, pred[256,512]{0,1:T(8,128)(4,1)S(1)} %get-tuple-element.142, f32[256,8,128]{2,0,1:T(8,128)S(1)} %get-tuple-element.147, f32[256,8]{0,1:T(8,128)S(1)} %get-tuple-element.230, ...), kind=kOutput, calls=%fused_computation.9 | convolution fusion | flops 274202624 | bytes 6569988 | tf_op jit(solution)/shard_map/while/body/eval_jaxpr/cond/branch_1_fun/ths,sd->thd/dot_general | solution.py:51
  104.9 0.8 fusion.26
  106.4 5.4 %conditional.3 = ((f32[256,8]{0,1:T(8,128)S(1)}, f32[256,8]{0,1:T(8,128)S(1)}, f32[256,8,128]{2,0,1:T(8,128)S(1)})) conditional(s32[]{:T(128)} %convert_element_type.27, (f32[256,8]{0,1:T(8,128)S(1)}, f32[256,8]{0,1:T(8,128)S(1)}, f32[256,8,128]{2,0,1:T(8,128)S(1)}) %tuple.45, (pred[256,512]{0,1:T(8,128)(4,1)S(1)}, s32[]{:T(128)}, ...), branch_computations={%region_2.2_spmd, %region_3.5_spmd} | conditional | flops 551030784 | bytes 15990858 | solution.py:62
  106.4 1.7 fusion.2
  108.1 1.0 fusion.4
  109.2 2.6 %fusion.8 = f32[256,8,128]{2,0,1:T(8,128)S(1)} fusion(f32[512,256,8]{1,0,2:T(8,128)S(1)} %get-tuple-element.234, f32[256,8]{0,1:T(8,128)S(1)} %max.7, pred[256,512]{0,1:T(8,128)(4,1)S(1)} %get-tuple-element.142, f32[256,8,128]{2,0,1:T(8,128)S(1)} %get-tuple-element.147, f32[256,8]{0,1:T(8,128)S(1)} %get-tuple-element.230, ...), kind=kOutput, calls=%fused_computation.9 | convolution fusion | flops 274202624 | bytes 6569988 | tf_op jit(solution)/shard_map/while/body/eval_jaxpr/cond/branch_1_fun/ths,sd->thd/dot_general | solution.py:51
  111.8 0.6 dynamic_slice.39
  113.1 0.8 fusion.26
  114.6 5.4 %conditional.3 = ((f32[256,8]{0,1:T(8,128)S(1)}, f32[256,8]{0,1:T(8,128)S(1)}, f32[256,8,128]{2,0,1:T(8,128)S(1)})) conditional(s32[]{:T(128)} %convert_element_type.27, (f32[256,8]{0,1:T(8,128)S(1)}, f32[256,8]{0,1:T(8,128)S(1)}, f32[256,8,128]{2,0,1:T(8,128)S(1)}) %tuple.45, (pred[256,512]{0,1:T(8,128)(4,1)S(1)}, s32[]{:T(128)}, ...), branch_computations={%region_2.2_spmd, %region_3.5_spmd} | conditional | flops 551030784 | bytes 15990858 | solution.py:62
  114.6 1.7 fusion.2
  116.4 1.0 fusion.4
  117.4 2.6 %fusion.8 = f32[256,8,128]{2,0,1:T(8,128)S(1)} fusion(f32[512,256,8]{1,0,2:T(8,128)S(1)} %get-tuple-element.234, f32[256,8]{0,1:T(8,128)S(1)} %max.7, pred[256,512]{0,1:T(8,128)(4,1)S(1)} %get-tuple-element.142, f32[256,8,128]{2,0,1:T(8,128)S(1)} %get-tuple-element.147, f32[256,8]{0,1:T(8,128)S(1)} %get-tuple-element.230, ...), kind=kOutput, calls=%fused_computation.9 | convolution fusion | flops 274202624 | bytes 6569988 | tf_op jit(solution)/shard_map/while/body/eval_jaxpr/cond/branch_1_fun/ths,sd->thd/dot_general | solution.py:51
  121.4 0.8 fusion.26
  122.8 5.4 %conditional.3 = ((f32[256,8]{0,1:T(8,128)S(1)}, f32[256,8]{0,1:T(8,128)S(1)}, f32[256,8,128]{2,0,1:T(8,128)S(1)})) conditional(s32[]{:T(128)} %convert_element_type.27, (f32[256,8]{0,1:T(8,128)S(1)}, f32[256,8]{0,1:T(8,128)S(1)}, f32[256,8,128]{2,0,1:T(8,128)S(1)}) %tuple.45, (pred[256,512]{0,1:T(8,128)(4,1)S(1)}, s32[]{:T(128)}, ...), branch_computations={%region_2.2_spmd, %region_3.5_spmd} | conditional | flops 551030784 | bytes 15990858 | solution.py:62
  122.9 1.7 fusion.2
  124.6 1.0 fusion.4
  125.7 2.6 %fusion.8 = f32[256,8,128]{2,0,1:T(8,128)S(1)} fusion(f32[512,256,8]{1,0,2:T(8,128)S(1)} %get-tuple-element.234, f32[256,8]{0,1:T(8,128)S(1)} %max.7, pred[256,512]{0,1:T(8,128)(4,1)S(1)} %get-tuple-element.142, f32[256,8,128]{2,0,1:T(8,128)S(1)} %get-tuple-element.147, f32[256,8]{0,1:T(8,128)S(1)} %get-tuple-element.230, ...), kind=kOutput, calls=%fused_computation.9 | convolution fusion | flops 274202624 | bytes 6569988 | tf_op jit(solution)/shard_map/while/body/eval_jaxpr/cond/branch_1_fun/ths,sd->thd/dot_general | solution.py:51
  128.3 0.6 dynamic_slice.39
  129.6 0.8 fusion.26
  131.1 5.4 %conditional.3 = ((f32[256,8]{0,1:T(8,128)S(1)}, f32[256,8]{0,1:T(8,128)S(1)}, f32[256,8,128]{2,0,1:T(8,128)S(1)})) conditional(s32[]{:T(128)} %convert_element_type.27, (f32[256,8]{0,1:T(8,128)S(1)}, f32[256,8]{0,1:T(8,128)S(1)}, f32[256,8,128]{2,0,1:T(8,128)S(1)}) %tuple.45, (pred[256,512]{0,1:T(8,128)(4,1)S(1)}, s32[]{:T(128)}, ...), branch_computations={%region_2.2_spmd, %region_3.5_spmd} | conditional | flops 551030784 | bytes 15990858 | solution.py:62
  131.1 1.7 fusion.2
  132.9 1.0 fusion.4
  133.9 2.6 %fusion.8 = f32[256,8,128]{2,0,1:T(8,128)S(1)} fusion(f32[512,256,8]{1,0,2:T(8,128)S(1)} %get-tuple-element.234, f32[256,8]{0,1:T(8,128)S(1)} %max.7, pred[256,512]{0,1:T(8,128)(4,1)S(1)} %get-tuple-element.142, f32[256,8,128]{2,0,1:T(8,128)S(1)} %get-tuple-element.147, f32[256,8]{0,1:T(8,128)S(1)} %get-tuple-element.230, ...), kind=kOutput, calls=%fused_computation.9 | convolution fusion | flops 274202624 | bytes 6569988 | tf_op jit(solution)/shard_map/while/body/eval_jaxpr/cond/branch_1_fun/ths,sd->thd/dot_general | solution.py:51
  137.8 0.8 fusion.26
  139.3 5.4 %conditional.3 = ((f32[256,8]{0,1:T(8,128)S(1)}, f32[256,8]{0,1:T(8,128)S(1)}, f32[256,8,128]{2,0,1:T(8,128)S(1)})) conditional(s32[]{:T(128)} %convert_element_type.27, (f32[256,8]{0,1:T(8,128)S(1)}, f32[256,8]{0,1:T(8,128)S(1)}, f32[256,8,128]{2,0,1:T(8,128)S(1)}) %tuple.45, (pred[256,512]{0,1:T(8,128)(4,1)S(1)}, s32[]{:T(128)}, ...), branch_computations={%region_2.2_spmd, %region_3.5_spmd} | conditional | flops 551030784 | bytes 15990858 | solution.py:62
  139.3 1.7 fusion.2
  141.1 1.0 fusion.4
  142.1 2.6 %fusion.8 = f32[256,8,128]{2,0,1:T(8,128)S(1)} fusion(f32[512,256,8]{1,0,2:T(8,128)S(1)} %get-tuple-element.234, f32[256,8]{0,1:T(8,128)S(1)} %max.7, pred[256,512]{0,1:T(8,128)(4,1)S(1)} %get-tuple-element.142, f32[256,8,128]{2,0,1:T(8,128)S(1)} %get-tuple-element.147, f32[256,8]{0,1:T(8,128)S(1)} %get-tuple-element.230, ...), kind=kOutput, calls=%fused_computation.9 | convolution fusion | flops 274202624 | bytes 6569988 | tf_op jit(solution)/shard_map/while/body/eval_jaxpr/cond/branch_1_fun/ths,sd->thd/dot_general | solution.py:51
  146.1 0.8 fusion.26
  147.6 5.4 %conditional.3 = ((f32[256,8]{0,1:T(8,128)S(1)}, f32[256,8]{0,1:T(8,128)S(1)}, f32[256,8,128]{2,0,1:T(8,128)S(1)})) conditional(s32[]{:T(128)} %convert_element_type.27, (f32[256,8]{0,1:T(8,128)S(1)}, f32[256,8]{0,1:T(8,128)S(1)}, f32[256,8,128]{2,0,1:T(8,128)S(1)}) %tuple.45, (pred[256,512]{0,1:T(8,128)(4,1)S(1)}, s32[]{:T(128)}, ...), branch_computations={%region_2.2_spmd, %region_3.5_spmd} | conditional | flops 551030784 | bytes 15990858 | solution.py:62
  147.6 1.7 fusion.2
  149.3 1.0 fusion.4
  150.4 2.6 %fusion.8 = f32[256,8,128]{2,0,1:T(8,128)S(1)} fusion(f32[512,256,8]{1,0,2:T(8,128)S(1)} %get-tuple-element.234, f32[256,8]{0,1:T(8,128)S(1)} %max.7, pred[256,512]{0,1:T(8,128)(4,1)S(1)} %get-tuple-element.142, f32[256,8,128]{2,0,1:T(8,128)S(1)} %get-tuple-element.147, f32[256,8]{0,1:T(8,128)S(1)} %get-tuple-element.230, ...), kind=kOutput, calls=%fused_computation.9 | convolution fusion | flops 274202624 | bytes 6569988 | tf_op jit(solution)/shard_map/while/body/eval_jaxpr/cond/branch_1_fun/ths,sd->thd/dot_general | solution.py:51
  154.3 0.8 fusion.26
  155.8 0.6 dynamic_slice.39
  157.2 0.8 fusion.26
  160.0 0.8 fusion.26
  162.8 0.8 fusion.26
  165.7 0.8 fusion.26
  168.5 0.8 fusion.26
  171.3 0.8 fusion.26
  172.8 1.1 copy_bitcast_fusion
  (108 shorter events, 9.6 us)
Async XLA Ops:
  6.5 13.7 %copy-start.1 = (bf16[256,1024]{1,0:T(8,128)(2,1)S(1)}, bf16[256,1024]{1,0:T(8,128)(2,1)}, u32[]{:S(2)}) copy-start(bf16[256,1024]{1,0:T(8,128)(2,1)} %param.8) | copy-start | bytes 1572868
  6.5 72.2 %all-gather.2.cloned.1.call-start = ((), (), s32[]{:S(2)}) async-start(), calls=%async_computation.1 | async-start | bytes 2162688 | tf_op jit(solution)/shard_map/all_gather | solution.py:105
  7.3 13.5 %copy-start = (s32[8192]{0:T(1024)S(1)}, s32[8192]{0:T(1024)}, u32[]{:S(2)}) copy-start(s32[8192]{0:T(1024)} %param.11) | copy-start | bytes 98308
  9.9 36.7 %all-to-all-start = ((bf16[32,256,128]{2,1,0:T(8,128)(2,1)}), bf16[32,256,128]{2,1,0:T(8,128)(2,1)}, u32[]{:S(2)}, u32[]{:S(2)}) async-start(bf16[32,256,128]{2,1,0:T(8,128)(2,1)} %stack.2), calls=%async_computation | async-start | bytes 4194304 | tf_op jit(solution)/shard_map/all_to_all | solution.py:11
Sparse Core Ops, SparseCore 0:
  10.5 68.2 all-gather.1
